TPU v7x, 256 devices: a whole 4x4x8 slice. The times are simulated.
256 devices in a mesh: orb: 8 (over z), ri: 8 (over y, core), pair: 4 (over x).
Axes of the slice: x: 4, y: 4, z: 8, core: 2. Of those that a mesh axis runs over, the one named last changes fastest.
Arguments:
- three_center: bfloat16 [4096, 64, 1024], P(('orb', 'ri', 'pair')), may hold values from -0.59765625 to 0.59765625
- block_dest: int32 [4096, 1], P('orb'), may hold values from 0 to 31; in each aligned block of 16 rows (0 to 15, 16 to 31, ...) at most 2 rows name the same one
- block_row: int32 [4096], P('orb'), may hold values from 0 to 7
- block_col: int32 [4096], P('orb'), may hold values from 0 to 7
- occ_density: bfloat16 [256, 256], P('orb'), may hold values from -0.375 to 0.375
- virt_density: bfloat16 [256, 256], P('orb'), may hold values from -0.375 to 0.375
- occ_mask: int32 [8, 8], P('orb'), may hold values 0 or 1
- virt_mask: int32 [8, 8], P('orb'), may hold values 0 or 1
Outputs:
- chi_slabs: float32 [16384, 64], P(('orb', 'ri', 'pair'))
Inputs may be any that keep to these rules, and one draw needn't show every extreme that they name: `block_dest`: in the 16 rows of one device, no owner is named by more than 2 rows.
All inputs are finite; a program needn't handle non-finite values. No bound on the sum of `occ_mask` or of `virt_mask` on one device may be relied on, other than what follows from the above.
Results may differ from a plain program's by a relative error of at most 0.0047.
Values may be sent and summed in bfloat16 or wider, within the bound.
No kernel may reach another device: no remote copies, remote signals or barrier semaphores. Data moves between devices by JAX's collectives and lax.ppermute only.
A program may use at most 192 MiB of HBM per device.

v0:
```python
import jax
import jax.numpy as jnp
from jax import lax
from jax.sharding import PartitionSpec as P

BR = 64
BA = 32


def expand(mask_blocks, block_width):
    return jnp.repeat(jnp.repeat(mask_blocks, block_width, axis=0), block_width, axis=1)


def body(
    three_center, block_dest, block_row, block_col, occ_density, virt_density, occ_mask, virt_mask
):
    owners = lax.axis_size(("ri", "pair"))
    owner_index = lax.axis_index(("ri", "pair"))
    blocks_dev = three_center.shape[0]
    slot_cap = max(2, (blocks_dev + owners - 1) // owners)
    slot_count = owners * slot_cap
    ao_blocks = occ_mask.shape[1]
    ao_width = occ_density.shape[1]
    all_dest = block_dest[:, 0].reshape(owners, blocks_dev)
    targets = jnp.arange(owners, dtype=jnp.int32)
    hit_table = (all_dest[:, :, None] == targets).astype(jnp.int32)
    rank_in_dest = jnp.sum(jnp.cumsum(hit_table, axis=1) * hit_table, axis=2) - 1
    positions = all_dest * slot_cap + rank_in_dest
    own_positions = lax.dynamic_index_in_dim(positions, owner_index, 0, keepdims=False)
    sources = (
        jnp.zeros((slot_count,), jnp.int32)
        .at[own_positions]
        .set(jnp.arange(blocks_dev, dtype=jnp.int32))
    )
    filled = jnp.zeros((slot_count,), jnp.bool_).at[own_positions].set(True)
    outgoing = jnp.where(
        filled[:, None, None],
        jnp.take(three_center, sources, axis=0),
        jnp.zeros((), three_center.dtype),
    )
    occ_local = occ_density * expand(occ_mask, BA).astype(jnp.bfloat16)
    virt_local = virt_density * expand(virt_mask, BA).astype(jnp.bfloat16)
    occ_whole, virt_whole = (
        lax.all_gather(occ_local, "orb", axis=0, tiled=True),
        lax.all_gather(virt_local, "orb", axis=0, tiled=True),
    )
    incoming = lax.all_to_all(outgoing, ("ri", "pair"), split_axis=0, concat_axis=0, tiled=True)
    arrival = targets[:, None] * slot_cap + rank_in_dest
    landing = jnp.where(all_dest == owner_index, arrival, slot_count).reshape(-1)
    cell_index = block_row * ao_blocks + block_col
    slot_cell = jnp.full((slot_count,), -1, jnp.int32).at[landing].set(cell_index, mode="drop")
    select_cells = (
        slot_cell[:, None] == jnp.arange(ao_blocks * ao_blocks, dtype=jnp.int32)
    ).astype(jnp.bfloat16)
    dense_flat = lax.dot_general(
        select_cells,
        incoming.reshape(slot_count, -1),
        (((0,), (0,)), ((), ())),
        preferred_element_type=jnp.float32,
    )
    dense_blocks = dense_flat.astype(jnp.bfloat16).reshape(ao_blocks, ao_blocks, BR, BA, BA)
    occ_rows = occ_whole.reshape(ao_blocks, BA, ao_width)
    virt_rows = virt_whole.reshape(ao_blocks, BA, ao_width)
    group_rows = BR // 2

    def one_group(block_index):
        part_dense = lax.dynamic_slice_in_dim(dense_blocks, block_index * group_rows, group_rows, 2)
        half_done = lax.dot_general(
            occ_rows, part_dense, (((0, 1), (0, 3)), ((), ())), preferred_element_type=jnp.float32
        ).astype(jnp.bfloat16)
        both_done = lax.dot_general(
            half_done, virt_rows, (((1, 3), (0, 1)), ((), ())), preferred_element_type=jnp.float32
        ).astype(jnp.bfloat16)
        both_five = both_done.reshape(ao_blocks, BA, group_rows, ao_blocks, BA)
        return lax.dot_general(
            both_five,
            dense_blocks,
            (((0, 1, 3, 4), (0, 3, 1, 4)), ((), ())),
            preferred_element_type=jnp.float32,
        )

    chi_parts = lax.map(one_group, jnp.arange(2, dtype=jnp.int32))
    return chi_parts.reshape(BR, BR)


def solution(mesh):
    placed = (
        P(("orb", "ri", "pair"), None, None),
        P("orb", None),
        P("orb"),
        P("orb"),
        P("orb", None),
        P("orb", None),
        P("orb", None),
        P("orb", None),
    )
    return jax.shard_map(
        body, mesh=mesh, in_specs=placed, out_specs=P(("orb", "ri", "pair"), None), check_vma=False
    )
```

profile of v0, /device:TPU:1, one launch (start us, length us, event | category | flops | bytes accessed | tf_op | source)
XLA Modules:
  0.0 486.6 jit_solution(3271578971000475231)
XLA Ops:
  0.0 0.0 copy-start
  0.0 0.5 broadcast.90
  0.5 1.5 reduce.5
  2.0 0.1 eq.38
  2.1 0.1 copy.23
  2.1 0.5 fusion.37
  2.7 0.2 fusion.29
  2.9 0.6 scatter_custom_fusion.2
  3.5 0.0 copy-done
  3.6 5.3 %gather_fusion = bf16[64,64,1024]{2,1,0:T(8,128)(2,1)} fusion(bf16[16,64,1024]{2,1,0:T(8,128)(2,1)S(1)} %copy-done, s32[1024]{0:T(1024)S(1)} %pad_clamp_fusion), kind=kCustom, calls=%fused_computation | custom fusion | bytes 16777472 | tf_op jit(solution)/shard_map/jit(_take)/gather | solution.py:38
  8.9 0.6 scatter_custom_fusion.1
  9.5 7.6 %select_select_fusion = bf16[64,64,1024]{2,1,0:T(8,128)(2,1)} fusion(bf16[64,64,1024]{2,1,0:T(8,128)(2,1)} %gather_fusion, pred[64]{0:T(512)(128)(4,1)S(1)} %compare_and_fusion, pred[64]{0:T(512)(128)(4,1)S(1)} %scatter_custom_fusion.1), kind=kLoop, calls=%fused_computation.18 | loop fusion | flops 8388608 | bytes 16777344 | tf_op jit(solution)/shard_map/jit(_where)/select_n | solution.py:36
  17.1 0.0 copy-start.6
  17.1 0.0 copy-start.2
  17.2 0.0 copy-start.3
  17.2 8.8 %all-to-all-start = ((bf16[64,64,1024]{2,1,0:T(8,128)(2,1)}), bf16[64,64,1024]{2,1,0:T(8,128)(2,1)}, u32[]{:S(2)}, u32[]{:S(2)}) async-start(bf16[64,64,1024]{2,1,0:T(8,128)(2,1)} %select_select_fusion), calls=%async_computation | async-start | bytes 16777216 | tf_op jit(solution)/shard_map/all_to_all | solution.py:47
  26.0 0.1 copy.24
  26.1 0.1 add.75
  26.1 0.0 copy-done.8
  26.2 0.1 broadcast_in_dim.74
  26.2 0.1 convert_element_type.42
  26.3 0.1 broadcast_in_dim.76
  26.4 0.1 convert_element_type.45
  26.5 0.0 copy-done.4
  26.5 2.4 scatter_custom_fusion
  29.0 0.0 copy-done.2
  29.0 24.7 %all_gather.6 = bf16[256,256]{1,0:T(8,128)(2,1)S(1)} all-gather(bf16[32,256]{1,0:T(8,128)(2,1)S(1)} %broadcast_multiply_fusion.1), channel_id=1, replica_groups=mesh['orb'=8,'ri'=8,'pair'=4] {'orb'}, dimensions={0}, use_global_device_ids=true | all-gather | bytes 147456 | tf_op jit(solution)/shard_map/all_gather | solution.py:44
  53.7 21.3 %all_gather.7 = bf16[256,256]{1,0:T(8,128)(2,1)S(1)} all-gather(bf16[32,256]{1,0:T(8,128)(2,1)S(1)} %broadcast_multiply_fusion), channel_id=1, replica_groups=mesh['orb'=8,'ri'=8,'pair'=4] {'orb'}, dimensions={0}, use_global_device_ids=true | all-gather | bytes 147456 | tf_op jit(solution)/shard_map/all_gather | solution.py:45
  74.9 50.0 %all-to-all-done = bf16[64,64,1024]{2,1,0:T(8,128)(2,1)} async-done(((bf16[64,64,1024]{2,1,0:T(8,128)(2,1)}), bf16[64,64,1024]{2,1,0:T(8,128)(2,1)}, u32[]{:S(2)}, u32[]{:S(2)}) %all-to-all-start) | async-done | bytes 8388640 | tf_op jit(solution)/shard_map/all_to_all | solution.py:47
  125.0 11.9 %copy.30 = bf16[8,8,64,1024]{3,1,2,0:T(8,128)(2,1)} copy(bf16[8,8,64,1024]{3,2,1,0:T(8,128)(2,1)} %bitcast.22) | data formatting | bytes 16777216
  136.9 9.1 %convolution_convert_fusion = bf16[64,65536]{1,0:T(8,128)(2,1)} fusion(bf16[64,65536]{1,0:T(8,128)(2,1)} %bitcast.67, s32[64]{0:T(128)S(1)} %scatter_custom_fusion), kind=kOutput, calls=%fused_computation.17 | convolution fusion | flops 541069312 | bytes 16777472 | tf_op jit(solution)/shard_map/dot_general | solution.py:55
  145.9 28.4 %reshape.101 = bf16[8,8,64,32,32]{4,3,2,1,0:T(8,128)(2,1)} reshape(bf16[64,65536]{1,0:T(8,128)(2,1)} %convolution_convert_fusion) | data formatting | bytes 16777216 | tf_op jit(solution)/shard_map/reshape | solution.py:61
  174.3 44.5 %copy.26 = bf16[8,8,64,32,32]{3,4,0,1,2:T(8,128)(2,1)} copy(bf16[8,8,64,32,32]{4,3,2,1,0:T(8,128)(2,1)} %reshape.101) | data formatting | bytes 16777216 | tf_op jit(solution)/shard_map/while | solution.py:82
  218.8 266.0 %while.10 = (s32[]{:T(128)}, f32[2,32,64]{2,1,0:T(8,128)S(1)}, s32[2]{0:T(128)S(1)}, bf16[8,8,64,32,32]{3,4,0,1,2:T(8,128)(2,1)}, bf16[8,32,256]{2,1,0:T(8,128)(...) while((s32[]{:T(128)}, f32[2,32,64]{2,1,0:T(8,128)S(1)}, ...), condition=%wide.region_6.7_spmd, body=%wide.region_5.6_spmd.sunk | while | flops 2420113408 | bytes 58998948 | solution.py:82
  234.3 0.7 dynamic_slice.31
  235.6 13.6 %bitcast_convert_fusion.3 = bf16[256,32,256]{2,0,1:T(8,128)(2,1)} fusion(bf16[8,8,64,32,32]{3,4,0,1,2:T(8,128)(2,1)} %get-tuple-element.136, s32[]{:T(128)S(6)} %select_n.61, bf16[8,32,256]{2,1,0:T(8,128)(2,1)S(1)} %get-tuple-element.138, bf16[8,32,256]{2,1,0:T(8,128)(2,1)S(1)} %get-tuple-element.137), kind=kOutput, calls=%fused_computation.8.clone.1 | convolution fusion | flops 2151677952 | bytes 21233668 | tf_op jit(solution)/shard_map/while/body/eval_jaxpr/dot_general | solution.py:71
  249.2 18.7 %reshape.160 = bf16[8,32,32,8,32]{4,3,1,0,2:T(8,128)(2,1)} reshape(bf16[256,32,256]{2,0,1:T(8,128)(2,1)} %bitcast_convert_fusion.3) | data formatting | bytes 8388608 | tf_op jit(solution)/shard_map/while/body/eval_jaxpr/reshape | solution.py:74
  267.9 52.5 %copy.40 = bf16[8,8,64,32,32]{2,4,1,3,0:T(8,128)(2,1)} copy(bf16[8,8,64,32,32]{3,4,0,1,2:T(8,128)(2,1)} %get-tuple-element.136) | data formatting | bytes 16777216 | tf_op jit(solution)/shard_map
  320.4 39.1 %fusion.53 = f32[2,32,64]{2,1,0:T(8,128)S(1)} fusion(f32[2,32,64]{2,1,0:T(8,128)S(1)} %get-tuple-element.124, s32[]{:T(128)} %get-tuple-element.123, bf16[8,8,64,32,32]{2,4,1,3,0:T(8,128)(2,1)} %copy.40, bf16[8,32,32,8,32]{4,3,1,0,2:T(8,128)(2,1)} %reshape.160), kind=kOutput, calls=%fused_computation.13.clone.1 | convolution fusion | flops 268435456 | bytes 12599300 | tf_op jit(solution)/shard_map/while/body/eval_jaxpr/dot_general | solution.py:75
  359.5 0.7 dynamic_slice.31
  360.9 13.6 %bitcast_convert_fusion.3 = bf16[256,32,256]{2,0,1:T(8,128)(2,1)} fusion(bf16[8,8,64,32,32]{3,4,0,1,2:T(8,128)(2,1)} %get-tuple-element.136, s32[]{:T(128)S(6)} %select_n.61, bf16[8,32,256]{2,1,0:T(8,128)(2,1)S(1)} %get-tuple-element.138, bf16[8,32,256]{2,1,0:T(8,128)(2,1)S(1)} %get-tuple-element.137), kind=kOutput, calls=%fused_computation.8.clone.1 | convolution fusion | flops 2151677952 | bytes 21233668 | tf_op jit(solution)/shard_map/while/body/eval_jaxpr/dot_general | solution.py:71
  374.5 18.7 %reshape.160 = bf16[8,32,32,8,32]{4,3,1,0,2:T(8,128)(2,1)} reshape(bf16[256,32,256]{2,0,1:T(8,128)(2,1)} %bitcast_convert_fusion.3) | data formatting | bytes 8388608 | tf_op jit(solution)/shard_map/while/body/eval_jaxpr/reshape | solution.py:74
  393.2 52.5 %copy.40 = bf16[8,8,64,32,32]{2,4,1,3,0:T(8,128)(2,1)} copy(bf16[8,8,64,32,32]{3,4,0,1,2:T(8,128)(2,1)} %get-tuple-element.136) | data formatting | bytes 16777216 | tf_op jit(solution)/shard_map
  445.6 39.1 %fusion.53 = f32[2,32,64]{2,1,0:T(8,128)S(1)} fusion(f32[2,32,64]{2,1,0:T(8,128)S(1)} %get-tuple-element.124, s32[]{:T(128)} %get-tuple-element.123, bf16[8,8,64,32,32]{2,4,1,3,0:T(8,128)(2,1)} %copy.40, bf16[8,32,32,8,32]{4,3,1,0,2:T(8,128)(2,1)} %reshape.160), kind=kOutput, calls=%fused_computation.13.clone.1 | convolution fusion | flops 268435456 | bytes 12599300 | tf_op jit(solution)/shard_map/while/body/eval_jaxpr/dot_general | solution.py:75
  484.8 0.0 copy-start.7
  484.8 0.0 copy-start.1
  484.8 0.6 copy-done.7
  485.4 1.0 copy-done.1
  (24 shorter events, 0.1 us)
Async XLA Ops:
  0.0 3.5 copy-start
  17.1 9.0 %copy-start.8 = (s32[1,8]{1,0:T(1,128)S(1)}, s32[1,8]{1,0:T(1,128)}, u32[]{:S(2)}) copy-start(s32[1,8]{1,0:T(1,128)} %param.16) | copy-start | bytes 100
  17.1 9.2 %copy-start.9 = (s32[1,8]{1,0:T(1,128)S(1)}, s32[1,8]{1,0:T(1,128)}, u32[]{:S(2)}) copy-start(s32[1,8]{1,0:T(1,128)} %param.17) | copy-start | bytes 100
  17.1 9.4 %copy-start.4 = (s32[512,1]{0,1:T(1,128)S(1)}, s32[512,1]{0,1:T(1,128)}, u32[]{:S(2)}) copy-start(s32[512,1]{0,1:T(1,128)} %param.11) | copy-start | bytes 6148
  17.1 9.4 %copy-start.5 = (s32[512]{0:T(512)S(1)}, s32[512]{0:T(512)}, u32[]{:S(2)}) copy-start(s32[512]{0:T(512)} %param.13) | copy-start | bytes 6148
  17.1 9.4 %copy-start.6 = (s32[512]{0:T(512)S(1)}, s32[512]{0:T(512)}, u32[]{:S(2)}) copy-start(s32[512]{0:T(512)} %param.12) | copy-start | bytes 6148
  17.1 11.8 %copy-start.2 = (bf16[32,256]{1,0:T(8,128)(2,1)S(1)}, bf16[32,256]{1,0:T(8,128)(2,1)}, u32[]{:S(2)}) copy-start(bf16[32,256]{1,0:T(8,128)(2,1)} %param.14) | copy-start | bytes 49156
  17.2 36.5 %copy-start.3 = (bf16[32,256]{1,0:T(8,128)(2,1)S(1)}, bf16[32,256]{1,0:T(8,128)(2,1)}, u32[]{:S(2)}) copy-start(bf16[32,256]{1,0:T(8,128)(2,1)} %param.15) | copy-start | bytes 49156
  17.2 107.8 %all-to-all-start = ((bf16[64,64,1024]{2,1,0:T(8,128)(2,1)}), bf16[64,64,1024]{2,1,0:T(8,128)(2,1)}, u32[]{:S(2)}, u32[]{:S(2)}) async-start(bf16[64,64,1024]{2,1,0:T(8,128)(2,1)} %select_select_fusion), calls=%async_computation | async-start | bytes 16777216 | tf_op jit(solution)/shard_map/all_to_all | solution.py:47
  484.8 0.6 copy-start.7
  484.8 1.6 copy-start.1
where the time goes:
time: 487 us
  local copies, waits for them, and re-layouts  240 us (49%)
  matrix products  114 us (23%)
  waiting for transfers between devices  50 us (10%)
  blocking collectives  45.9 us (9%)
  loops' own time  16.9 us (3%)
  other arithmetic  9.84 us (2%)
  starting transfers between devices  8.79 us (2%)
    another operation x3, local copies, waits for them, and re-layouts  105 us
    dot_general x2, matrix products, one_group(): lax.dot_general(both_five, dense_blocks, (((0, 1, 3, 4), (0, 3, 1, 4)), (...  78.3 us
    all_to_all x1, waiting for transfers between devices, body(): lax.all_to_all(outgoing, ('ri', 'pair'), split_axis=0, concat_axis=0, til...  50 us
    while x1, local copies, waits for them, and re-layouts, body(): chi_parts = lax.map(one_group, jnp.arange(2, dtype=jnp.int32))  44.5 us
    reshape x2, local copies, waits for them, and re-layouts, one_group(): both_five = both_done.reshape(ao_blocks, BA, group_rows, ao_blocks, BA)  37.4 us
    reshape x1, local copies, waits for them, and re-layouts, body(): dense_flat.astype(jnp.bfloat16).reshape(ao_blocks, ao_blocks, BR, BA, BA)  28.4 us
    dot_general x2, matrix products, one_group(): lax.dot_general(half_done, virt_rows, (((1, 3), (0, 1)), ((), ())), prefe...  27.2 us
    all_gather x1, blocking collectives, body(): lax.all_gather(occ_local, 'orb', axis=0, tiled=True)  24.7 us
  transfers between devices with their start and end apart: 1, of which 1 were waited for; matrix products, arithmetic and copies ran while one was open for 1% of the time, Pallas kernels for 0%

commit v1 on v0

v1 whole, which is shorter than its diff:
```python
import functools

import jax
import jax.numpy as jnp
from jax import lax
from jax.experimental import pallas as pl
from jax.experimental.pallas import tpu as pltpu
from jax.sharding import PartitionSpec as P

BR = 64
BA = 32
CAP = 2
LANES = 128


def expand(mask_blocks, block_width):
    return jnp.repeat(jnp.repeat(mask_blocks, block_width, axis=0), block_width, axis=1)


def pack_kernel(owners, blocks_dev, me_ref, dest_ref, blocks_ref, out_ref, taken_ref, sem):
    me = me_ref[0]

    def clear(o, _):
        taken_ref[o] = 0
        return 0

    lax.fori_loop(0, owners, clear, 0)

    def send(k, _):
        owner = dest_ref[me * blocks_dev + k]
        rank = taken_ref[owner]
        taken_ref[owner] = rank + 1
        pltpu.make_async_copy(blocks_ref.at[k], out_ref.at[owner * CAP + rank], sem).start()
        return 0

    lax.fori_loop(0, blocks_dev, send, 0)
    pltpu.make_async_copy(blocks_ref, out_ref.at[pl.ds(0, blocks_dev)], sem).wait()


def pack(me, dest, blocks, owners):
    blocks_dev = blocks.shape[0]
    return pl.pallas_call(
        functools.partial(pack_kernel, owners, blocks_dev),
        out_shape=jax.ShapeDtypeStruct((owners * CAP,) + blocks.shape[1:], blocks.dtype),
        in_specs=[
            pl.BlockSpec(memory_space=pltpu.SMEM),
            pl.BlockSpec(memory_space=pltpu.SMEM),
            pl.BlockSpec(memory_space=pl.ANY),
        ],
        out_specs=pl.BlockSpec(memory_space=pl.ANY),
        scratch_shapes=[pltpu.SMEM((owners,), jnp.int32), pltpu.SemaphoreType.DMA],
        name="pack",
    )(me, dest, blocks)


def plan_kernel(owners, blocks_dev, ao_blocks, me_ref, dest_ref, row_ref, col_ref, cell_ref, next_ref, list_ref):
    me = me_ref[0]
    slots = owners * CAP
    cells = ao_blocks * ao_blocks

    def clear(c, _):
        cell_ref[c] = slots
        return 0

    lax.fori_loop(0, cells, clear, 0)

    def source(s, total):
        def block(k, carry):
            rank, total = carry
            index = s * blocks_dev + k
            mine = dest_ref[index] == me

            @pl.when(mine)
            def _():
                slot = s * CAP + rank
                cell = row_ref[index] * ao_blocks + col_ref[index]
                next_ref[slot] = cell_ref[cell]
                cell_ref[cell] = slot
                list_ref[1 + total] = slot

            step = mine.astype(jnp.int32)
            return rank + step, total + step

        return lax.fori_loop(0, blocks_dev, block, (jnp.int32(0), total))[1]

    list_ref[0] = lax.fori_loop(0, owners, source, jnp.int32(0))


def plan(me, dest, row, col, owners, blocks_dev, ao_blocks):
    smem = pl.BlockSpec(memory_space=pltpu.SMEM)
    slots = owners * CAP
    return pl.pallas_call(
        functools.partial(plan_kernel, owners, blocks_dev, ao_blocks),
        out_shape=(
            jax.ShapeDtypeStruct((ao_blocks * ao_blocks,), jnp.int32),
            jax.ShapeDtypeStruct((slots,), jnp.int32),
            jax.ShapeDtypeStruct((slots + 1,), jnp.int32),
        ),
        in_specs=[smem] * 4,
        out_specs=(smem,) * 3,
        name="plan",
    )(me, dest, row, col)


def slab_kernel(
    slots, ao_blocks, cell_ref, next_ref, list_ref, occ_ref, virt_ref, recv_ref, out_ref,
    held, dense, work, total, sem,
):
    count = list_ref[0]
    width = ao_blocks * BA
    per_tile = LANES // BA

    def fetch(i, _):
        slot = list_ref[1 + i]
        pltpu.make_async_copy(recv_ref.at[slot], held.at[slot], sem).start()
        return 0

    lax.fori_loop(0, count, fetch, 0)
    held[slots] = jnp.zeros(held.shape[1:], held.dtype)

    def arrive(i, _):
        pltpu.make_async_copy(recv_ref.at[0], held.at[0], sem).wait()
        return 0

    lax.fori_loop(0, count, arrive, 0)

    def merge(c, _):
        first = cell_ref[c]

        @pl.when(first < slots)
        def _():
            second = next_ref[first]

            @pl.when(second < slots)
            def _():
                total[...] = held[first].astype(jnp.float32)

                def add(slot):
                    total[...] += held[slot].astype(jnp.float32)
                    return next_ref[slot]

                lax.while_loop(lambda slot: slot < slots, add, second)
                held[first] = total[...].astype(held.dtype)

        return 0

    lax.fori_loop(0, ao_blocks * ao_blocks, merge, 0)

    group = lax.broadcasted_iota(jnp.int32, (BR, LANES), 1) // BA
    low_half = group < 2
    even = group % 2 == 0
    tiles = width // LANES

    def place(step, _):
        r = step // tiles
        tile = step % tiles
        lanes = pl.ds(pl.multiple_of(tile * LANES, LANES), LANES)
        sources = [cell_ref[r * ao_blocks + tile * per_tile + j] for j in range(per_tile)]
        for hi in range(BA // per_tile):
            x = [held[s, :, hi * LANES : (hi + 1) * LANES].astype(jnp.float32) for s in sources]
            z = [None] * 4
            for a, b in ((0, 2), (1, 3)):
                z[a] = jnp.where(low_half, x[a], pltpu.roll(x[b], 64, 1))
                z[b] = jnp.where(low_half, pltpu.roll(x[a], 64, 1), x[b])
            y = [None] * 4
            for a, b in ((0, 1), (2, 3)):
                y[a] = jnp.where(even, z[a], pltpu.roll(z[b], 32, 1))
                y[b] = jnp.where(even, pltpu.roll(z[a], 96, 1), z[b])
            for j in range(per_tile):
                mu = r * BA + hi * per_tile + j
                work[tile, pl.ds(pl.multiple_of(mu * BR, BR), BR), :] = y[j]
                dense[mu, :, lanes] = y[j].astype(jnp.bfloat16)
        return 0

    lax.fori_loop(0, ao_blocks * tiles, place, 0)

    occ_t = occ_ref[...]
    virt = virt_ref[...]

    def transform(p, _):
        rows = pl.ds(p, width, stride=BR)
        part = jnp.concatenate([work[t, rows, :] for t in range(tiles)], axis=1).astype(jnp.bfloat16)
        half = jnp.dot(occ_t, part, preferred_element_type=jnp.float32).astype(jnp.bfloat16)
        both = jnp.dot(half, virt, preferred_element_type=jnp.float32)
        for t in range(tiles):
            work[t, rows, :] = both[:, t * LANES : (t + 1) * LANES]
        return 0

    lax.fori_loop(0, BR, transform, 0)

    def contract(i, acc):
        for j in range(4):
            mu = i * 4 + j
            rows = pl.ds(pl.multiple_of(mu * BR, BR), BR)
            both = jnp.concatenate([work[t, rows, :] for t in range(tiles)], axis=1).astype(jnp.bfloat16)
            acc = acc + lax.dot_general(
                both, dense[mu], (((1,), (1,)), ((), ())), preferred_element_type=jnp.float32
            )
        return acc

    out_ref[...] = lax.fori_loop(0, width // 4, contract, jnp.zeros((BR, BR), jnp.float32))


def slab(cell, chain, listed, occ_t, virt, recv, ao_blocks):
    slots = recv.shape[0]
    width = ao_blocks * BA
    smem = pl.BlockSpec(memory_space=pltpu.SMEM)
    vmem = pl.BlockSpec(memory_space=pltpu.VMEM)
    return pl.pallas_call(
        functools.partial(slab_kernel, slots, ao_blocks),
        out_shape=jax.ShapeDtypeStruct((BR, BR), jnp.float32),
        in_specs=[smem, smem, smem, vmem, vmem, pl.BlockSpec(memory_space=pl.ANY)],
        out_specs=vmem,
        scratch_shapes=[
            pltpu.VMEM((slots + 1, BR, BA * BA), jnp.bfloat16),
            pltpu.VMEM((width, BR, width), jnp.bfloat16),
            pltpu.VMEM((width // LANES, width * BR, LANES), jnp.float32),
            pltpu.VMEM((BR, BA * BA), jnp.float32),
            pltpu.SemaphoreType.DMA,
        ],
        compiler_params=pltpu.CompilerParams(vmem_limit_bytes=48 * 1024 * 1024),
        name="slab",
    )(cell, chain, listed, occ_t, virt, recv)


def body(
    three_center, block_dest, block_row, block_col, occ_density, virt_density, occ_mask, virt_mask
):
    owners = lax.axis_size(("ri", "pair"))
    blocks_dev = three_center.shape[0]
    ao_blocks = occ_mask.shape[1]
    width = occ_density.shape[1]
    me = lax.axis_index(("ri", "pair")).astype(jnp.int32).reshape(1)
    dest = block_dest.reshape(-1)
    outgoing = pack(me, dest, three_center, owners)
    incoming = lax.all_to_all(outgoing, ("ri", "pair"), split_axis=0, concat_axis=0, tiled=True)
    local = jnp.concatenate(
        [
            occ_density * expand(occ_mask, BA).astype(jnp.bfloat16),
            virt_density * expand(virt_mask, BA).astype(jnp.bfloat16),
        ],
        axis=1,
    )
    whole = lax.all_gather(local, "orb", axis=0, tiled=True)
    cell, chain, listed = plan(me, dest, block_row, block_col, owners, blocks_dev, ao_blocks)
    return slab(cell, chain, listed, whole[:, :width].T, whole[:, width:], incoming, ao_blocks)


def solution(mesh):
    placed = (
        P(("orb", "ri", "pair"), None, None),
        P("orb", None),
        P("orb"),
        P("orb"),
        P("orb", None),
        P("orb", None),
        P("orb", None),
        P("orb", None),
    )
    return jax.shard_map(
        body, mesh=mesh, in_specs=placed, out_specs=P(("orb", "ri", "pair"), None), check_vma=False
    )
```

time: 487 us -> 253 us (0.52)
  local copies, waits for them, and re-layouts: 240 us -> 2.4 us
  Pallas kernels: 0 us -> 152 us
  matrix products: 114 us -> 0 us
  blocking collectives: 45.9 us -> 25 us
  loops' own time: 16.9 us -> 0 us
  waiting for transfers between devices: 50 us -> 63.3 us
  other arithmetic: 9.84 us -> 0.02 us
    pallas_call x0 -> x3, Pallas kernels: none -> 152 us  [the longest x1 76.6 us: slab(): pl.pallas_call(functools.partial(slab_kernel, slots, ao_blocks), out_shap...]
    dot_general x5 -> x0, matrix products: 114 us -> none  [the longest x2 78.3 us: one_group(): lax.dot_general(both_five, dense_blocks, (((0, 1, 3, 4), (0, 3, 1, 4)), (...]
    another operation x3 -> x0, local copies, waits for them, and re-layouts: 105 us -> none
    reshape x3 -> x0, local copies, waits for them, and re-layouts: 65.8 us -> none  [the longest x2 37.4 us: one_group(): both_five = both_done.reshape(ao_blocks, BA, group_rows, ao_blocks, BA)]
    while x1 -> x0, local copies, waits for them, and re-layouts: 44.5 us -> none  [body(): chi_parts = lax.map(one_group, jnp.arange(2, dtype=jnp.int32))]
    all_gather x2 -> x1, blocking collectives: 45.9 us -> 25 us  [body(): whole = lax.all_gather(local, 'orb', axis=0, tiled=True)]
    another operation x1 -> x0, loops' own time: 16.9 us -> none  [body(): chi_parts = lax.map(one_group, jnp.arange(2, dtype=jnp.int32))]
    all_to_all x1, waiting for transfers between devices: 50 us -> 63.3 us  [body(): lax.all_to_all(outgoing, ('ri', 'pair'), split_axis=0, concat_axis=0, til...]
  transfers between devices with their start and end apart: 1 -> 1, of which waited for: 1 -> 1; matrix products, arithmetic and copies ran while one was open for 1% -> 0% of each run, Pallas kernels for 0% -> 4%
where the time goes in v1:
time: 253 us; the launch traced here: 252 us
  Pallas kernels  152 us (60%)
  waiting for transfers between devices  63.3 us (25%)
  blocking collectives  25 us (10%)
  starting transfers between devices  8.79 us (3%)
    pallas_call x1, Pallas kernels, slab(): pl.pallas_call(functools.partial(slab_kernel, slots, ao_blocks), out_shap...  76.6 us
    pallas_call x1, Pallas kernels, pack(): pl.pallas_call(functools.partial(pack_kernel, owners, blocks_dev), out_sh...  65.5 us
    all_to_all x1, waiting for transfers between devices, body(): lax.all_to_all(outgoing, ('ri', 'pair'), split_axis=0, concat_axis=0, til...  63.3 us
    all_gather x1, blocking collectives, body(): whole = lax.all_gather(local, 'orb', axis=0, tiled=True)  25 us
    pallas_call x1, Pallas kernels, plan(): pl.pallas_call(functools.partial(plan_kernel, owners, blocks_dev, ao_bloc...  10.2 us
    all_to_all x1, starting transfers between devices, body(): lax.all_to_all(outgoing, ('ri', 'pair'), split_axis=0, concat_axis=0, til...  8.79 us
  transfers between devices with their start and end apart: 1, of which 1 were waited for; matrix products, arithmetic and copies ran while one was open for 0% of the time, Pallas kernels for 4%

profile of v1, /device:TPU:1, one launch (start us, length us, event | category | flops | bytes accessed | tf_op | source)
XLA Modules:
  0.0 251.9 jit_solution(6135482153991743583)
XLA Ops:
  0.0 65.5 %pack.1 = bf16[64,64,1024]{2,1,0:T(8,128)(2,1)} custom-call(s32[1]{0:T(128)} %bitcast.me_ref, s32[512]{0:T(512)} %bitcast.8, bf16[16,64,1024]{2,1,0:T(8,128)(2,1)} %blocks_ref.1), custom_call_target="tpu_custom_call" | custom-call | tf_op jit(solution)/shard_map/pack/pallas_call | solution.py:42
  65.5 0.0 copy-start.5
  65.6 0.0 copy-start.6
  65.6 0.0 copy-start.3
  65.6 0.0 copy-start.4
  65.6 8.8 %all-to-all-start = ((bf16[64,64,1024]{2,1,0:T(8,128)(2,1)}), bf16[64,64,1024]{2,1,0:T(8,128)(2,1)}, u32[]{:S(2)}, u32[]{:S(2)}) async-start(bf16[64,64,1024]{2,1,0:T(8,128)(2,1)} %pack.1), calls=%async_computation | async-start | bytes 16777216 | tf_op jit(solution)/shard_map/all_to_all | solution.py:236
  74.4 0.0 copy-done.5
  74.4 0.1 broadcast_in_dim.12
  74.5 0.1 convert_element_type.24
  74.6 0.0 copy-done.6
  74.6 0.1 broadcast_in_dim.14
  74.7 0.1 convert_element_type.27
  74.7 0.0 copy-done.3
  74.7 0.0 copy-done.4
  74.8 25.0 %all_gather.3 = bf16[256,512]{1,0:T(8,128)(2,1)S(1)} all-gather(bf16[32,512]{1,0:T(8,128)(2,1)S(1)} %pad_maximum_fusion), channel_id=1, replica_groups=mesh['orb'=8,'ri'=8,'pair'=4] {'orb'}, dimensions={0}, use_global_device_ids=true | all-gather | bytes 294912 | tf_op jit(solution)/shard_map/all_gather | solution.py:244
  99.8 0.1 copy.9.occ_ref
  99.9 10.2 %plan.1 = (s32[64]{0:T(128)}, s32[64]{0:T(128)}, s32[65]{0:T(128)}) custom-call(s32[1]{0:T(128)} %bitcast.me_ref, s32[512]{0:T(512)} %bitcast.9, s32[512]{0:T(512)} %row_ref.1, s32[512]{0:T(512)} %col_ref.1), custom_call_target="tpu_custom_call" | custom-call | tf_op jit(solution)/shard_map/plan/pallas_call | solution.py:92
  110.1 63.3 %all-to-all-done.recv_ref = bf16[64,64,1024]{2,1,0:T(8,128)(2,1)} async-done(((bf16[64,64,1024]{2,1,0:T(8,128)(2,1)}), bf16[64,64,1024]{2,1,0:T(8,128)(2,1)}, u32[]{:S(2)}, u32[]{:S(2)}) %all-to-all-start) | async-done | bytes 8388640 | tf_op jit(solution)/shard_map/all_to_all | solution.py:236
  173.4 0.0 copy-start
  173.4 0.6 copy-done
  174.0 0.0 copy-start.1
  174.0 0.7 copy-done.1
  174.7 0.0 copy-start.2
  174.7 0.7 copy-done.2
  175.3 76.6 %slab.1 = f32[64,64]{1,0:T(8,128)} custom-call(s32[64]{0:T(128)S(1)} %copy-done, s32[64]{0:T(128)S(1)} %copy-done.1, s32[65]{0:T(128)S(1)} %copy-done.2, bf16[256,256]{1,0:T(8,128)(2,1)S(1)} %copy.9.occ_ref, bf16[256,256]{1,0:T(8,128)(2,1)S(1)} %get-tuple-element.11.virt_ref, bf16[64,64,1024]{2,1,0:T(8,128)(2,1)} %all-to-all-done.recv_ref), custom_call_target="tpu_custom_call" | custom-call | tf_op jit(solution)/shard_map/slab/pallas_call | solution.py:209
  (5 shorter events, 0.0 us)
Async XLA Ops:
  65.5 8.8 %copy-start.5 = (s32[1,8]{1,0:T(1,128)S(1)}, s32[1,8]{1,0:T(1,128)}, u32[]{:S(2)}) copy-start(s32[1,8]{1,0:T(1,128)} %param.14) | copy-start | bytes 100
  65.6 9.0 %copy-start.6 = (s32[1,8]{1,0:T(1,128)S(1)}, s32[1,8]{1,0:T(1,128)}, u32[]{:S(2)}) copy-start(s32[1,8]{1,0:T(1,128)} %param.15) | copy-start | bytes 100
  65.6 9.2 %copy-start.3 = (bf16[32,256]{1,0:T(8,128)(2,1)S(1)}, bf16[32,256]{1,0:T(8,128)(2,1)}, u32[]{:S(2)}) copy-start(bf16[32,256]{1,0:T(8,128)(2,1)} %param.13) | copy-start | bytes 49156
  65.6 9.2 %copy-start.4 = (bf16[32,256]{1,0:T(8,128)(2,1)S(1)}, bf16[32,256]{1,0:T(8,128)(2,1)}, u32[]{:S(2)}) copy-start(bf16[32,256]{1,0:T(8,128)(2,1)} %param.12) | copy-start | bytes 49156
  65.6 107.8 %all-to-all-start = ((bf16[64,64,1024]{2,1,0:T(8,128)(2,1)}), bf16[64,64,1024]{2,1,0:T(8,128)(2,1)}, u32[]{:S(2)}, u32[]{:S(2)}) async-start(bf16[64,64,1024]{2,1,0:T(8,128)(2,1)} %pack.1), calls=%async_computation | async-start | bytes 16777216 | tf_op jit(solution)/shard_map/all_to_all | solution.py:236
  173.4 0.6 copy-start
  174.0 0.7 copy-start.1
  174.7 0.7 copy-start.2

commit v2 on v1

v2 whole, which is shorter than its diff:
```python
import functools

import jax
import jax.numpy as jnp
from jax import lax
from jax.experimental import pallas as pl
from jax.experimental.pallas import tpu as pltpu
from jax.sharding import PartitionSpec as P

BR = 64
BA = 32
CAP = 2
LANES = 128
PITCH = BR + 1


def expand(mask_blocks, block_width):
    return jnp.repeat(jnp.repeat(mask_blocks, block_width, axis=0), block_width, axis=1)


def pack_kernel(owners, blocks_dev, me_ref, dest_ref, blocks_ref, out_ref, taken_ref, sem):
    me = me_ref[0]

    def clear(o, _):
        taken_ref[o] = 0
        return 0

    lax.fori_loop(0, owners, clear, 0)

    def send(k, _):
        owner = dest_ref[me * blocks_dev + k]
        rank = taken_ref[owner]
        taken_ref[owner] = rank + 1
        pltpu.make_async_copy(blocks_ref.at[k], out_ref.at[owner * CAP + rank], sem).start()
        return 0

    lax.fori_loop(0, blocks_dev, send, 0)
    pltpu.make_async_copy(blocks_ref, out_ref.at[pl.ds(0, blocks_dev)], sem).wait()


def pack(me, dest, blocks, owners):
    blocks_dev = blocks.shape[0]
    return pl.pallas_call(
        functools.partial(pack_kernel, owners, blocks_dev),
        out_shape=jax.ShapeDtypeStruct((owners * CAP,) + blocks.shape[1:], blocks.dtype),
        in_specs=[
            pl.BlockSpec(memory_space=pltpu.SMEM),
            pl.BlockSpec(memory_space=pltpu.SMEM),
            pl.BlockSpec(memory_space=pltpu.VMEM),
        ],
        out_specs=pl.BlockSpec(memory_space=pl.ANY),
        scratch_shapes=[pltpu.SMEM((owners,), jnp.int32), pltpu.SemaphoreType.DMA],
        name="pack",
    )(me, dest, blocks)


def plan_kernel(owners, blocks_dev, ao_blocks, me_ref, dest_ref, row_ref, col_ref, table_ref):
    me = me_ref[0]
    slots = owners * CAP
    cells = ao_blocks * ao_blocks

    def clear(c, _):
        table_ref[c] = slots
        return 0

    lax.fori_loop(0, cells, clear, 0)

    def source(s, total):
        def block(k, carry):
            rank, total = carry
            index = s * blocks_dev + k
            mine = dest_ref[index] == me

            @pl.when(mine)
            def _():
                slot = s * CAP + rank
                cell = row_ref[index] * ao_blocks + col_ref[index]
                table_ref[cells + slot] = table_ref[cell]
                table_ref[cell] = slot
                table_ref[cells + slots + 1 + total] = slot

            step = mine.astype(jnp.int32)
            return rank + step, total + step

        return lax.fori_loop(0, blocks_dev, block, (jnp.int32(0), total))[1]

    table_ref[cells + slots] = lax.fori_loop(0, owners, source, jnp.int32(0))


def plan(me, dest, row, col, owners, blocks_dev, ao_blocks):
    smem = pl.BlockSpec(memory_space=pltpu.SMEM)
    slots = owners * CAP
    return pl.pallas_call(
        functools.partial(plan_kernel, owners, blocks_dev, ao_blocks),
        out_shape=jax.ShapeDtypeStruct((ao_blocks * ao_blocks + 2 * slots + 1,), jnp.int32),
        in_specs=[smem] * 4,
        out_specs=smem,
        name="plan",
    )(me, dest, row, col)


def slab_kernel(
    slots, ao_blocks, table_ref, occ_ref, virt_ref, shuffle_ref, recv_ref, out_ref,
    held, dense, work, total, sem,
):
    width = ao_blocks * BA
    cells = ao_blocks * ao_blocks
    per_tile = LANES // BA
    tiles = width // LANES
    count = table_ref[cells + slots]

    def fetch(i, _):
        slot = table_ref[cells + slots + 1 + i]
        pltpu.make_async_copy(recv_ref.at[slot], held.at[slot], sem).start()
        return 0

    lax.fori_loop(0, count, fetch, 0)
    held[slots] = jnp.zeros(held.shape[1:], held.dtype)

    def arrive(i, _):
        pltpu.make_async_copy(recv_ref.at[0], held.at[0], sem).wait()
        return 0

    lax.fori_loop(0, count, arrive, 0)

    def merge(c, _):
        first = table_ref[c]

        @pl.when(first < slots)
        def _():
            second = table_ref[cells + first]

            @pl.when(second < slots)
            def _():
                total[...] = held[first].astype(jnp.float32)

                def add(slot):
                    total[...] += held[slot].astype(jnp.float32)
                    return table_ref[cells + slot]

                lax.while_loop(lambda slot: slot < slots, add, second)
                held[first] = total[...].astype(held.dtype)

        return 0

    lax.fori_loop(0, cells, merge, 0)

    shuffle = shuffle_ref[...]

    def place(step, _):
        r = step // tiles
        tile = step % tiles
        lanes = pl.ds(pl.multiple_of(tile * LANES, LANES), LANES)
        sources = [table_ref[r * ao_blocks + tile * per_tile + j] for j in range(per_tile)]
        x = jnp.concatenate(
            [
                jnp.concatenate([held[s, :, hi * LANES : (hi + 1) * LANES] for s in sources], axis=1)
                for hi in range(BA // per_tile)
            ],
            axis=0,
        )
        y = jnp.dot(x, shuffle, preferred_element_type=jnp.float32)
        for hi in range(BA // per_tile):
            for j in range(per_tile):
                mu = r * BA + hi * per_tile + j
                part = y[hi * BR : (hi + 1) * BR, j * LANES : (j + 1) * LANES]
                work[tile, pl.ds(mu * PITCH, BR), :] = part
                dense[mu, :, lanes] = part.astype(jnp.bfloat16)
        return 0

    lax.fori_loop(0, ao_blocks * tiles, place, 0)

    occ_t = occ_ref[...]
    virt = virt_ref[...]

    def transform(i, _):
        for j in range(8):
            rows = pl.ds(i * 8 + j, width, stride=PITCH)
            part = jnp.concatenate([work[t, rows, :] for t in range(tiles)], axis=1).astype(jnp.bfloat16)
            half = jnp.dot(occ_t, part, preferred_element_type=jnp.float32).astype(jnp.bfloat16)
            both = jnp.dot(half, virt, preferred_element_type=jnp.float32)
            for t in range(tiles):
                work[t, rows, :] = both[:, t * LANES : (t + 1) * LANES]
        return 0

    lax.fori_loop(0, BR // 8, transform, 0)

    def contract(i, acc):
        left, right = [], []
        for j in range(16):
            mu = i * 16 + j
            left += [work[t, pl.ds(mu * PITCH, BR), :] for t in range(tiles)]
            right.append(dense[mu])
        return acc + lax.dot_general(
            jnp.concatenate(left, axis=1).astype(jnp.bfloat16),
            jnp.concatenate(right, axis=1),
            (((1,), (1,)), ((), ())),
            preferred_element_type=jnp.float32,
        )

    out_ref[...] = lax.fori_loop(0, width // 16, contract, jnp.zeros((BR, BR), jnp.float32))


def slab(table, occ_t, virt, recv, ao_blocks):
    slots = recv.shape[0]
    width = ao_blocks * BA
    per_tile = LANES // BA
    smem = pl.BlockSpec(memory_space=pltpu.SMEM)
    vmem = pl.BlockSpec(memory_space=pltpu.VMEM)
    eye = jnp.eye(per_tile, dtype=jnp.bfloat16)
    shuffle = jnp.einsum("ac,bd,vw->abvdcw", eye, eye, jnp.eye(BA, dtype=jnp.bfloat16))
    shuffle = shuffle.reshape(per_tile * LANES, per_tile * LANES)
    return pl.pallas_call(
        functools.partial(slab_kernel, slots, ao_blocks),
        out_shape=jax.ShapeDtypeStruct((BR, BR), jnp.float32),
        in_specs=[smem, vmem, vmem, vmem, pl.BlockSpec(memory_space=pl.ANY)],
        out_specs=vmem,
        scratch_shapes=[
            pltpu.VMEM((slots + 1, BR, BA * BA), jnp.bfloat16),
            pltpu.VMEM((width, BR, width), jnp.bfloat16),
            pltpu.VMEM((width // LANES, width * PITCH, LANES), jnp.float32),
            pltpu.VMEM((BR, BA * BA), jnp.float32),
            pltpu.SemaphoreType.DMA,
        ],
        compiler_params=pltpu.CompilerParams(vmem_limit_bytes=48 * 1024 * 1024),
        name="slab",
    )(table, occ_t, virt, shuffle, recv)


def body(
    three_center, block_dest, block_row, block_col, occ_density, virt_density, occ_mask, virt_mask
):
    owners = lax.axis_size(("ri", "pair"))
    blocks_dev = three_center.shape[0]
    ao_blocks = occ_mask.shape[1]
    width = occ_density.shape[1]
    me = lax.axis_index(("ri", "pair")).astype(jnp.int32).reshape(1)
    dest = block_dest.reshape(-1)
    outgoing = pack(me, dest, three_center, owners)
    incoming = lax.all_to_all(outgoing, ("ri", "pair"), split_axis=0, concat_axis=0, tiled=True)
    local = jnp.concatenate(
        [
            occ_density * expand(occ_mask, BA).astype(jnp.bfloat16),
            virt_density * expand(virt_mask, BA).astype(jnp.bfloat16),
        ],
        axis=1,
    )
    whole = lax.all_gather(local, "orb", axis=0, tiled=True)
    table = plan(me, dest, block_row, block_col, owners, blocks_dev, ao_blocks)
    return slab(table, whole[:, :width].T, whole[:, width:], incoming, ao_blocks)


def solution(mesh):
    placed = (
        P(("orb", "ri", "pair"), None, None),
        P("orb", None),
        P("orb"),
        P("orb"),
        P("orb", None),
        P("orb", None),
        P("orb", None),
        P("orb", None),
    )
    return jax.shard_map(
        body, mesh=mesh, in_specs=placed, out_specs=P(("orb", "ri", "pair"), None), check_vma=False
    )
```

time: 253 us -> 136 us (0.54)
  Pallas kernels: 152 us -> 35.6 us
  waiting for transfers between devices: 63.3 us -> 59.9 us
    pallas_call x1, Pallas kernels: 65.5 us -> 3.19 us  [pack(): pl.pallas_call(functools.partial(pack_kernel, owners, blocks_dev), out_sh...]
    pallas_call x1, Pallas kernels: 76.6 us -> 22 us  [slab(): pl.pallas_call(functools.partial(slab_kernel, slots, ao_blocks), out_shap...]
    all_to_all x1, waiting for transfers between devices: 63.3 us -> 59.9 us  [body(): lax.all_to_all(outgoing, ('ri', 'pair'), split_axis=0, concat_axis=0, til...]
  transfers between devices with their start and end apart: 1 -> 1, of which waited for: 1 -> 1; matrix products, arithmetic and copies ran while one was open for 0% -> 3% of each run, Pallas kernels for 4% -> 8%
where the time goes in v2:
time: 136 us; the launch traced here: 134 us
  waiting for transfers between devices  59.9 us (44%)
  Pallas kernels  35.6 us (26%)
  blocking collectives  25.1 us (18%)
  starting transfers between devices  8.71 us (6%)
  local copies, waits for them, and re-layouts  3.2 us (2%)
    all_to_all x1, waiting for transfers between devices, body(): lax.all_to_all(outgoing, ('ri', 'pair'), split_axis=0, concat_axis=0, til...  59.9 us
    all_gather x1, blocking collectives, body(): whole = lax.all_gather(local, 'orb', axis=0, tiled=True)  25.1 us
    pallas_call x1, Pallas kernels, slab(): pl.pallas_call(functools.partial(slab_kernel, slots, ao_blocks), out_shap...  22 us
    pallas_call x1, Pallas kernels, plan(): pl.pallas_call(functools.partial(plan_kernel, owners, blocks_dev, ao_bloc...  10.5 us
    all_to_all x1, starting transfers between devices, body(): lax.all_to_all(outgoing, ('ri', 'pair'), split_axis=0, concat_axis=0, til...  8.71 us
    pallas_call x1, Pallas kernels, pack(): pl.pallas_call(functools.partial(pack_kernel, owners, blocks_dev), out_sh...  3.19 us
  transfers between devices with their start and end apart: 1, of which 1 were waited for; matrix products, arithmetic and copies ran while one was open for 3% of the time, Pallas kernels for 8%

profile of v2, /device:TPU:1, one launch (start us, length us, event | category | flops | bytes accessed | tf_op | source)
XLA Modules:
  0.0 133.6 jit_solution(3369489005927387061)
XLA Ops:
  0.0 3.2 %pack.1 = bf16[64,64,1024]{2,1,0:T(8,128)(2,1)} custom-call(s32[1]{0:T(128)} %bitcast.me_ref, s32[512]{0:T(512)} %bitcast.10, bf16[16,64,1024]{2,1,0:T(8,128)(2,1)} %blocks_ref.1), custom_call_target="tpu_custom_call" | custom-call | tf_op jit(solution)/shard_map/pack/pallas_call | solution.py:43
  3.2 0.0 copy-start.3
  3.2 0.0 copy-start.4
  3.2 0.0 copy-start.1
  3.2 0.0 copy-start.2
  3.3 8.7 %all-to-all-start = ((bf16[64,64,1024]{2,1,0:T(8,128)(2,1)}), bf16[64,64,1024]{2,1,0:T(8,128)(2,1)}, u32[]{:S(2)}, u32[]{:S(2)}) async-start(bf16[64,64,1024]{2,1,0:T(8,128)(2,1)} %pack.1), calls=%async_computation | async-start | bytes 16777216 | tf_op jit(solution)/shard_map/all_to_all | solution.py:240
  12.0 0.0 copy-done.3
  12.0 0.1 broadcast_in_dim.12
  12.1 0.1 convert_element_type.26
  12.1 0.0 copy-done.4
  12.2 0.1 broadcast_in_dim.14
  12.2 0.1 convert_element_type.29
  12.3 0.0 copy-done.1
  12.3 0.0 copy-done.2
  12.4 25.1 %all_gather.3 = bf16[256,512]{1,0:T(8,128)(2,1)S(1)} all-gather(bf16[32,512]{1,0:T(8,128)(2,1)S(1)} %pad_maximum_fusion), channel_id=1, replica_groups=mesh['orb'=8,'ri'=8,'pair'=4] {'orb'}, dimensions={0}, use_global_device_ids=true | all-gather | bytes 294912 | tf_op jit(solution)/shard_map/all_gather | solution.py:248
  37.5 0.1 copy.9.occ_ref
  37.6 0.1 broadcast_multiply_fusion
  37.7 0.8 multiply_bitcast_fusion
  38.5 2.1 %reshape.23.shuffle_ref = bf16[512,512]{1,0:T(8,128)(2,1)S(1)} reshape(bf16[4,4,32,4,4,32]{5,4,3,2,1,0:T(4,128)(2,1)S(1)} %multiply_bitcast_fusion) | data formatting | bytes 1048576 | tf_op jit(solution)/shard_map/reshape | solution.py:212
  40.6 10.5 %plan.1.table_ref = s32[193]{0:T(256)} custom-call(s32[1]{0:T(128)} %bitcast.me_ref, s32[512]{0:T(512)} %bitcast.11, s32[512]{0:T(512)} %row_ref.1, s32[512]{0:T(512)} %col_ref.1), custom_call_target="tpu_custom_call" | custom-call | tf_op jit(solution)/shard_map/plan/pallas_call | solution.py:93
  51.1 59.9 %all-to-all-done.recv_ref = bf16[64,64,1024]{2,1,0:T(8,128)(2,1)} async-done(((bf16[64,64,1024]{2,1,0:T(8,128)(2,1)}), bf16[64,64,1024]{2,1,0:T(8,128)(2,1)}, u32[]{:S(2)}, u32[]{:S(2)}) %all-to-all-start) | async-done | bytes 8388640 | tf_op jit(solution)/shard_map/all_to_all | solution.py:240
  111.0 0.0 copy-start
  111.0 0.7 copy-done
  111.6 22.0 %slab.1 = f32[64,64]{1,0:T(8,128)} custom-call(s32[193]{0:T(256)S(1)} %copy-done, bf16[256,256]{1,0:T(8,128)(2,1)S(1)} %copy.9.occ_ref, bf16[256,256]{1,0:T(8,128)(2,1)S(1)} %get-tuple-element.5.virt_ref, bf16[512,512]{1,0:T(8,128)(2,1)S(1)} %reshape.23.shuffle_ref, bf16[64,64,1024]{2,1,0:T(8,128)(2,1)} %all-to-all-done.recv_ref), custom_call_target="tpu_custom_call" | custom-call | tf_op jit(solution)/shard_map/slab/pallas_call | solution.py:213
  (7 shorter events, 0.1 us)
Async XLA Ops:
  3.2 8.8 %copy-start.3 = (s32[1,8]{1,0:T(1,128)S(1)}, s32[1,8]{1,0:T(1,128)}, u32[]{:S(2)}) copy-start(s32[1,8]{1,0:T(1,128)} %param.14) | copy-start | bytes 100
  3.2 8.9 %copy-start.4 = (s32[1,8]{1,0:T(1,128)S(1)}, s32[1,8]{1,0:T(1,128)}, u32[]{:S(2)}) copy-start(s32[1,8]{1,0:T(1,128)} %param.15) | copy-start | bytes 100
  3.2 9.1 %copy-start.1 = (bf16[32,256]{1,0:T(8,128)(2,1)S(1)}, bf16[32,256]{1,0:T(8,128)(2,1)}, u32[]{:S(2)}) copy-start(bf16[32,256]{1,0:T(8,128)(2,1)} %param.13) | copy-start | bytes 49156
  3.2 9.1 %copy-start.2 = (bf16[32,256]{1,0:T(8,128)(2,1)S(1)}, bf16[32,256]{1,0:T(8,128)(2,1)}, u32[]{:S(2)}) copy-start(bf16[32,256]{1,0:T(8,128)(2,1)} %param.12) | copy-start | bytes 49156
  3.3 107.7 %all-to-all-start = ((bf16[64,64,1024]{2,1,0:T(8,128)(2,1)}), bf16[64,64,1024]{2,1,0:T(8,128)(2,1)}, u32[]{:S(2)}, u32[]{:S(2)}) async-start(bf16[64,64,1024]{2,1,0:T(8,128)(2,1)} %pack.1), calls=%async_computation | async-start | bytes 16777216 | tf_op jit(solution)/shard_map/all_to_all | solution.py:240
  111.0 0.7 copy-start
